TPU v7x, 1024 devices: a whole 4x4x32 slice. The times are simulated.
1024 devices in a mesh: gx: 4 (over x), gy: 8 (over y, core), ch: 32 (over z).
Axes of the slice: x: 4, y: 4, z: 32, core: 2. Of those that a mesh axis runs over, the one named last changes fastest.
Arguments:
- inputs: bfloat16 [16, 32, 32, 256], P('gx', 'gy', None, 'ch'), may hold values from -6 to 6
- weight: bfloat16 [3, 3, 3, 256, 256], P(None, None, None, 'ch'), may hold values from -0.125 to 0.125
- bias: bfloat16 [256], P('ch'), may hold values from -3 to 3
- cotangent: bfloat16 [16, 32, 32, 256], P('gx', 'gy', None, 'ch'), may hold values from -6 to 6
Outputs:
- activation: bfloat16 [16, 32, 32, 256], P('gx', 'gy', None, 'ch')
- input_grad: bfloat16 [16, 32, 32, 256], P('gx', 'gy', None, 'ch')
- weight_grad: float32 [3, 3, 3, 256, 256], P(None, None, None, 'ch')
- bias_grad: float32 [256], P('ch')
All inputs are finite; a program needn't handle non-finite values.
Results may differ from a plain program's by a relative error of at most 0.0075.
Values may be sent and summed in bfloat16 or wider, within the bound.
A program may use at most 32 MiB of HBM per device.

v0:
```python
import math

import jax
import jax.numpy as jnp
from jax import lax
from jax.sharding import PartitionSpec as P


def with_halo(x, sides, width):
    for axis, dim in sides:
        devices, length = (lax.axis_size(axis), x.shape[dim])
        up = [(i, (i + 1) % devices) for i in range(devices - 1)]
        down = [(j, i) for i, j in up]
        last = lax.slice_in_dim(x, length - width, length, axis=dim)
        initial = lax.slice_in_dim(x, 0, width, axis=dim)
        before = lax.ppermute(last, axis, up)
        after = lax.ppermute(initial, axis, down)
        x = jnp.concatenate([before, x, after], axis=dim)
    return x


def body(inputs, weight, bias, cotangent):
    span_x, span_y, span_z, local_ch = inputs.shape
    widest = weight.shape[4]
    local_cells = span_x * span_y * span_z
    offsets = [(a, b, c) for a in range(3) for b in range(3) for c in range(3)]
    depth_pad = ((0, 0), (0, 0), (1, 1), (0, 0))
    rimmed = with_halo(inputs, (("gx", 0), ("gy", 1)), 1)
    padded = jnp.pad(rimmed, depth_pad)
    blocks = []
    for a, b, c in offsets:
        blocks.append(
            padded[a : a + span_x, b : b + span_y, c : c + span_z].reshape(local_cells, local_ch)
        )
    patches = jnp.concatenate(blocks, axis=1)
    flat_weight = weight.reshape(27 * local_ch, widest)
    summed = lax.psum_scatter(
        lax.dot_general(
            flat_weight, patches, (((0,), (1,)), ((), ())), preferred_element_type=jnp.float32
        ),
        "ch",
        scatter_dimension=0,
        tiled=True,
    ).T
    summed = summed + bias.astype(jnp.float32)[None, :]
    activation = jax.nn.silu(summed).astype(jnp.bfloat16).reshape(span_x, span_y, span_z, local_ch)
    sigmoid_pre = jax.nn.sigmoid(summed)
    slope = (
        cotangent.reshape(local_cells, local_ch).astype(jnp.float32)
        * sigmoid_pre
        * (1.0 + summed * (1.0 - sigmoid_pre))
    ).astype(jnp.bfloat16)
    local_bias = jnp.sum(slope.astype(jnp.float32), axis=0)
    slope_grid = slope.reshape(span_x, span_y, span_z, local_ch)
    weight_turned = jnp.transpose(weight.reshape(27, local_ch, widest), (0, 2, 1))
    slope_rimmed = with_halo(slope_grid, (("gx", 0), ("gy", 1)), 1)
    piece = lax.all_gather(slope_rimmed, "ch", axis=3, tiled=True)
    back_sum = jnp.zeros((local_cells, local_ch), jnp.float32)
    amount = piece.shape[3]
    running = back_sum
    extended = jnp.pad(piece, depth_pad)
    tap_amount = extended.shape[3]
    for index, (a, b, c) in enumerate(offsets):
        a, b, c = (2 - a, 2 - b, 2 - c)
        cut = extended[a : a + span_x, b : b + span_y, c : c + span_z].reshape(
            local_cells, tap_amount
        )
        running = running + jnp.dot(cut, weight_turned[index], preferred_element_type=jnp.float32)
    back_sum = running
    interior = piece[1 : 1 + span_x, 1 : 1 + span_y].reshape(local_cells, amount)
    product = lax.dot_general(
        patches, interior, (((0,), (0,)), ((), ())), preferred_element_type=jnp.float32
    )
    kernel_sum = product
    back_sum, kernel_sum = (back_sum, kernel_sum)
    total_cells = local_cells * lax.axis_size("gx") * lax.axis_size("gy")
    factor = 1.0 / math.sqrt(total_cells)
    kernel_total, bias_total = lax.psum((kernel_sum * factor, local_bias * factor), ("gx", "gy"))
    input_grad = back_sum.astype(jnp.bfloat16).reshape(span_x, span_y, span_z, local_ch)
    return (activation, input_grad, kernel_total.reshape(3, 3, 3, local_ch, widest), bias_total)


def solution(mesh):
    return jax.shard_map(
        body,
        mesh=mesh,
        in_specs=(
            P("gx", "gy", None, "ch"),
            P(None, None, None, "ch", None),
            P("ch"),
            P("gx", "gy", None, "ch"),
        ),
        out_specs=(
            P("gx", "gy", None, "ch"),
            P("gx", "gy", None, "ch"),
            P(None, None, None, "ch", None),
            P("ch"),
        ),
        check_vma=False,
    )
```

profile of v0, /device:TPU:1, one launch (start us, length us, event | category | flops | bytes accessed | tf_op | source)
XLA Modules:
  0.0 499.9 jit_solution(16629264917501690745)
XLA Ops:
  7.2 0.7 fusion.24
  7.9 3.9 collective-permute-start
  11.9 1.3 collective-permute-start.1
  13.2 3.1 collective-permute-done.1
  16.3 0.9 pad_maximum_fusion.2
  17.2 5.2 %collective-permute-start.2 = (bf16[6,1,32,8]{2,3,1,0:T(8,128)(2,1)S(1)}, bf16[6,1,32,8]{2,3,1,0:T(8,128)(2,1)S(1)}, u32[]{:S(2)}, u32[]{:S(2)}) collective-permute-start(bf16[6,1,32,8]{2,3,1,0:T(8,128)(2,1)S(1)} %get-tuple-element.82), channel_id=1, source_target_pairs={{0,32},{32,64},{64,96},{96,128},{128,160},{160,192},{192,224},{1,3... | collective-permute-start | bytes 9224 | tf_op jit(solution)/shard_map/ppermute | solution.py:16
  22.4 10.7 %collective-permute-start.3 = (bf16[6,1,32,8]{2,3,1,0:T(8,128)(2,1)S(1)}, bf16[6,1,32,8]{2,3,1,0:T(8,128)(2,1)S(1)}, u32[]{:S(2)}, u32[]{:S(2)}) collective-permute-start(bf16[6,1,32,8]{2,3,1,0:T(8,128)(2,1)S(1)} %get-tuple-element.83), channel_id=1, source_target_pairs={{32,0},{64,32},{96,64},{128,96},{160,128},{192,160},{224,192},{33,... | collective-permute-start | bytes 9224 | tf_op jit(solution)/shard_map/ppermute | solution.py:17
  33.0 0.8 copy.130
  37.7 0.7 copy-done.8
  38.4 0.3 convolution_bitcast_fusion
  38.7 1.0 copy.161
  39.9 109.3 %reduce-scatter.4.cloned.1.call-done = f32[8,512]{1,0:T(8,128)} async-done(((f32[256,512]{1,0:T(8,128)}), f32[8,512]{1,0:T(8,128)}) %reduce-scatter.4.cloned.1.call-update) | async-done | bytes 16400 | tf_op jit(solution)/shard_map/reduce_scatter | solution.py:37
  149.2 0.9 convert_reduce_fusion
  150.2 3.1 collective-permute-start.4
  153.5 1.3 collective-permute-start.5
  154.9 3.5 collective-permute-done.5
  158.3 28.1 %collective-permute-start.6 = (bf16[6,1,32,8]{2,3,1,0:T(8,128)(2,1)S(1)}, bf16[6,1,32,8]{2,3,1,0:T(8,128)(2,1)S(1)}, u32[]{:S(2)}, u32[]{:S(2)}) collective-permute-start(bf16[6,1,32,8]{2,3,1,0:T(8,128)(2,1)S(1)} %get-tuple-element.77), channel_id=1, source_target_pairs={{0,32},{32,64},{64,96},{96,128},{128,160},{160,192},{192,224},{1,3... | collective-permute-start | bytes 9224 | tf_op jit(solution)/shard_map/ppermute | solution.py:16
  186.4 1.9 collective-permute-start.7
  188.4 61.3 %psum.15 = f32[8]{0:T(128)} all-reduce(f32[8]{0:T(128)S(1)} %broadcast_multiply_fusion), channel_id=1, replica_groups=mesh['gx'=4,'gy'=8,'ch'=32] {'gx','gy'}, use_global_device_ids=true, to_apply=%region_3.4 | all-reduce | flops 8 | bytes 64 | tf_op jit(solution)/shard_map/psum | solution.py:78
  249.8 0.6 copy.159
  250.4 55.8 %all_gather.3 = bf16[6,6,32,256]{2,3,1,0:T(8,128)(2,1)S(1)} all-gather(bf16[6,6,32,8]{2,3,1,0:T(8,128)(2,1)S(1)} %pad_maximum_fusion), channel_id=1, replica_groups=mesh['gx'=4,'gy'=8,'ch'=32] {'ch'}, dimensions={3}, use_global_device_ids=true | all-gather | bytes 608256 | tf_op jit(solution)/shard_map/all_gather | solution.py:57
  306.2 0.9 copy.149
  307.1 1.1 fusion.20
  308.2 2.3 pad_slice_fusion
  310.5 0.9 convolution_multiply_fusion
  311.5 1.2 fusion.18
  312.7 1.2 convolution_add_fusion.25
  313.9 1.1 convolution_add_fusion.24
  315.0 1.1 convolution_add_fusion.23
  316.1 1.1 convolution_add_fusion.22
  317.3 1.1 convolution_add_fusion.21
  318.4 1.1 convolution_add_fusion.20
  319.6 1.1 convolution_add_fusion.19
  320.7 0.2 convolution_add_fusion.18
  320.9 0.2 convolution_add_fusion.17
  321.1 0.2 convolution_add_fusion.16
  321.2 0.2 convolution_add_fusion.15
  321.4 0.2 convolution_add_fusion.14
  321.6 0.2 convolution_add_fusion.13
  321.8 0.2 convolution_add_fusion.12
  322.0 0.2 convolution_add_fusion.11
  322.2 0.2 convolution_add_fusion.10
  322.4 0.2 convolution_add_fusion.9
  322.5 0.2 convolution_add_fusion.8
  324.0 0.2 fusion
  324.3 0.6 copy.160
  324.9 166.5 %all-reduce.4.cloned.1.call-done = f32[3,3,3,8,256]{4,3,2,1,0:T(8,128)} async-done(((f32[3,3,3,8,256]{4,3,2,1,0:T(8,128)}), f32[3,3,3,8,256]{4,3,2,1,0:T(8,128)}) %all-reduce.4.cloned.1.call-update) | async-done | bytes 221200 | tf_op jit(solution)/shard_map/psum | solution.py:78
  491.4 1.6 copy.195
  (147 shorter events, 5.6 us)
Async XLA Ops:
  7.2 142.0 %reduce-scatter.4.cloned.1.call-start = ((), (), s32[]{:S(2)}) async-start(), calls=%async_computation.2 | async-start | bytes 540672 | tf_op jit(solution)/shard_map/reduce_scatter | solution.py:37
  7.9 5.2 %collective-permute-start = (bf16[1,4,32,8]{2,3,1,0:T(8,128)(2,1)S(1)}, bf16[1,4,32,8]{2,3,1,0:T(8,128)(2,1)S(1)}, u32[]{:S(2)}, u32[]{:S(2)}) collective-permute-start(bf16[1,4,32,8]{2,3,1,0:T(8,128)(2,1)S(1)} %get-tuple-element.88), channel_id=1, source_target_pairs={{0,256},{256,512},{512,768},{1,257},{257,513},{513,769},{2,258},{2... | collective-permute-start | bytes 6152 | tf_op jit(solution)/shard_map/ppermute | solution.py:16
  11.9 4.4 collective-permute-start.1
  17.2 17.0 %collective-permute-start.2 = (bf16[6,1,32,8]{2,3,1,0:T(8,128)(2,1)S(1)}, bf16[6,1,32,8]{2,3,1,0:T(8,128)(2,1)S(1)}, u32[]{:S(2)}, u32[]{:S(2)}) collective-permute-start(bf16[6,1,32,8]{2,3,1,0:T(8,128)(2,1)S(1)} %get-tuple-element.82), channel_id=1, source_target_pairs={{0,32},{32,64},{64,96},{96,128},{128,160},{160,192},{192,224},{1,3... | collective-permute-start | bytes 9224 | tf_op jit(solution)/shard_map/ppermute | solution.py:16
  22.4 11.8 %collective-permute-start.3 = (bf16[6,1,32,8]{2,3,1,0:T(8,128)(2,1)S(1)}, bf16[6,1,32,8]{2,3,1,0:T(8,128)(2,1)S(1)}, u32[]{:S(2)}, u32[]{:S(2)}) collective-permute-start(bf16[6,1,32,8]{2,3,1,0:T(8,128)(2,1)S(1)} %get-tuple-element.83), channel_id=1, source_target_pairs={{32,0},{64,32},{96,64},{128,96},{160,128},{192,160},{224,192},{33,... | collective-permute-start | bytes 9224 | tf_op jit(solution)/shard_map/ppermute | solution.py:17
  34.0 4.4 copy-start.10
  35.3 4.4 copy-start.13
  35.3 4.4 copy-start.12
  37.7 0.7 copy-start.8
  39.7 451.7 %all-reduce.4.cloned.1.call-start = ((), (), s32[]{:S(2)}) async-start(), calls=%async_computation.1 | async-start | bytes 442368 | tf_op jit(solution)/shard_map/psum | solution.py:78
  150.2 4.6 collective-permute-start.4
  153.5 4.8 collective-permute-start.5
  158.3 92.1 %collective-permute-start.6 = (bf16[6,1,32,8]{2,3,1,0:T(8,128)(2,1)S(1)}, bf16[6,1,32,8]{2,3,1,0:T(8,128)(2,1)S(1)}, u32[]{:S(2)}, u32[]{:S(2)}) collective-permute-start(bf16[6,1,32,8]{2,3,1,0:T(8,128)(2,1)S(1)} %get-tuple-element.77), channel_id=1, source_target_pairs={{0,32},{32,64},{64,96},{96,128},{128,160},{160,192},{192,224},{1,3... | collective-permute-start | bytes 9224 | tf_op jit(solution)/shard_map/ppermute | solution.py:16
  186.4 64.0 %collective-permute-start.7 = (bf16[6,1,32,8]{2,3,1,0:T(8,128)(2,1)S(1)}, bf16[6,1,32,8]{2,3,1,0:T(8,128)(2,1)S(1)}, u32[]{:S(2)}, u32[]{:S(2)}) collective-permute-start(bf16[6,1,32,8]{2,3,1,0:T(8,128)(2,1)S(1)} %get-tuple-element.78), channel_id=1, source_target_pairs={{32,0},{64,32},{96,64},{128,96},{160,128},{192,160},{224,192},{33,... | collective-permute-start | bytes 9224 | tf_op jit(solution)/shard_map/ppermute | solution.py:17
  308.2 2.3 copy-start.9
  310.5 6.8 %copy-start.11 = (bf16[3,3,3,8,256]{4,3,2,1,0:T(8,128)(2,1)S(1)}, bf16[3,3,3,8,256]{4,3,2,1,0:T(8,128)(2,1)}, u32[]{:S(2)}) copy-start(bf16[3,3,3,8,256]{4,3,2,1,0:T(8,128)(2,1)} %param.5) | copy-start | bytes 331780
  310.5 10.6 %copy-start.2 = (bf16[4,4,32,256]{3,2,1,0:T(8,128)(2,1)S(1)}, bf16[4,4,32,256]{3,2,1,0:T(8,128)(2,1)}, u32[]{:S(2)}) copy-start(bf16[4,4,32,256]{3,2,1,0:T(8,128)(2,1)} %get-tuple-element.48) | copy-start | bytes 786436
  311.4 10.6 %copy-start.1 = (bf16[4,4,32,256]{3,2,1,0:T(8,128)(2,1)S(1)}, bf16[4,4,32,256]{3,2,1,0:T(8,128)(2,1)}, u32[]{:S(2)}) copy-start(bf16[4,4,32,256]{3,2,1,0:T(8,128)(2,1)} %get-tuple-element.36) | copy-start | bytes 786436
  311.4 9.3 %copy-start.7 = (bf16[4,4,32,256]{3,2,1,0:T(8,128)(2,1)S(1)}, bf16[4,4,32,256]{3,2,1,0:T(8,128)(2,1)}, u32[]{:S(2)}) copy-start(bf16[4,4,32,256]{3,2,1,0:T(8,128)(2,1)} %get-tuple-element.31) | copy-start | bytes 786436
  311.4 9.4 %copy-start.6 = (bf16[4,4,32,256]{3,2,1,0:T(8,128)(2,1)S(1)}, bf16[4,4,32,256]{3,2,1,0:T(8,128)(2,1)}, u32[]{:S(2)}) copy-start(bf16[4,4,32,256]{3,2,1,0:T(8,128)(2,1)} %get-tuple-element.32) | copy-start | bytes 786436
  311.4 9.8 %copy-start.5 = (bf16[4,4,32,256]{3,2,1,0:T(8,128)(2,1)S(1)}, bf16[4,4,32,256]{3,2,1,0:T(8,128)(2,1)}, u32[]{:S(2)}) copy-start(bf16[4,4,32,256]{3,2,1,0:T(8,128)(2,1)} %get-tuple-element.33) | copy-start | bytes 786436
  311.5 10.0 %copy-start.4 = (bf16[4,4,32,256]{3,2,1,0:T(8,128)(2,1)S(1)}, bf16[4,4,32,256]{3,2,1,0:T(8,128)(2,1)}, u32[]{:S(2)}) copy-start(bf16[4,4,32,256]{3,2,1,0:T(8,128)(2,1)} %get-tuple-element.34) | copy-start | bytes 786436
  311.5 10.3 %copy-start.3 = (bf16[4,4,32,256]{3,2,1,0:T(8,128)(2,1)S(1)}, bf16[4,4,32,256]{3,2,1,0:T(8,128)(2,1)}, u32[]{:S(2)}) copy-start(bf16[4,4,32,256]{3,2,1,0:T(8,128)(2,1)} %get-tuple-element.35) | copy-start | bytes 786436
  312.7 9.7 %copy-start = (bf16[4,4,32,256]{3,2,1,0:T(8,128)(2,1)S(1)}, bf16[4,4,32,256]{3,2,1,0:T(8,128)(2,1)}, u32[]{:S(2)}) copy-start(bf16[4,4,32,256]{3,2,1,0:T(8,128)(2,1)} %get-tuple-element.37) | copy-start | bytes 786436
Sparse Core Ops, SparseCore 0:
  39.8 109.3 reduce-scatter.3
  311.5 179.8 all-reduce.3
where the time goes:
time: 501 us; the launch traced here: 500 us
  waiting for transfers between devices  282 us (56%)
  blocking collectives  117 us (23%)
  starting transfers between devices  55.6 us (11%)
  between operations  14.7 us (3%)
  local copies, waits for them, and re-layouts  14.4 us (3%)
  matrix products  13.9 us (3%)
    psum x1, waiting for transfers between devices, body(): lax.psum((kernel_sum * factor, local_bias * factor), ('gx', 'gy'))  166 us
    reduce_scatter x1, waiting for transfers between devices, body(): lax.psum_scatter(lax.dot_general(flat_weight, patches, (((0,), (1,)), (()...  109 us
    psum x1, blocking collectives, body(): lax.psum((kernel_sum * factor, local_bias * factor), ('gx', 'gy'))  61.3 us
    all_gather x1, blocking collectives, body(): piece = lax.all_gather(slope_rimmed, 'ch', axis=3, tiled=True)  55.8 us
    ppermute x4, starting transfers between devices, with_halo(): before = lax.ppermute(last, axis, up)  40.3 us
    ppermute x4, starting transfers between devices, with_halo(): after = lax.ppermute(initial, axis, down)  15.2 us
    dot_general x27, matrix products, body(): jnp.dot(cut, weight_turned[index], preferred_element_type=jnp.float32)  12.7 us
  transfers between devices with their start and end apart: 10, of which 4 were waited for; matrix products, arithmetic and copies ran while one was open for 3% of the time, Pallas kernels for 0%

commit v1 on v0

v1 whole, which is shorter than its diff:
```python
import functools
import math

import jax
import jax.numpy as jnp
from jax import lax
from jax.experimental import pallas as pl
from jax.experimental.pallas import tpu as pltpu
from jax.sharding import PartitionSpec as P

MESH = pl.DeviceIdType.MESH
CLASSES = 4
HALO = [(dx, dy) for dx in (-1, 0, 1) for dy in (-1, 0, 1) if (dx, dy) != (0, 0)]
F32 = jnp.float32
BF16 = jnp.bfloat16


def kernel(
    nx, ny, nz, factor,
    x_ref, w_ref, bias_ref, cot_ref,
    act_ref, ig_ref, wg_ref, bg_ref,
    planes, rim, part, near, acc, far, gath, grad, pieces, total, back, back_in,
    halo_s, halo_r, rs1_s, rs1_r, rs2_s, rs2_r, ag1_s, ag1_r, ag2_s, ag2_r,
    wr_s, wr_r, wa_s, wa_r, bk_s, bk_r,
):
    ix, iy, iz = lax.axis_index("gx"), lax.axis_index("gy"), lax.axis_index("ch")
    groups = nz // CLASSES
    half = groups // 2
    peers = nx * ny
    chans = 8 * nz
    cls, grp = lax.rem(iz, CLASSES), lax.div(iz, CLASSES)

    def at_xy(dx, dy):
        return (lax.rem(ix + dx + nx, nx), lax.rem(iy + dy + ny, ny), iz)

    def at_z(dz):
        return (ix, iy, lax.rem(iz + dz + nz, nz))

    barrier = pltpu.get_barrier_semaphore()

    def greet(device):
        pl.semaphore_signal(barrier, inc=1, device_id=device, device_id_type=MESH)

    @pl.loop(1, peers)
    def _(k):
        greet(at_xy(lax.div(k, ny), lax.rem(k, ny)))

    strides = [1, nz - 1, 2, nz - 2] + [CLASSES * k for k in range(1, groups)]
    for dz in strides:
        greet(at_z(dz))

    lane = lax.broadcasted_iota(jnp.int32, (8, 128), 1)
    depth = lax.rem(lane, 32)

    def joined(ref, x):
        return jnp.concatenate([ref[x, y].astype(F32) for y in range(4)], axis=1)

    for x in range(4):
        planes[x] = joined(x_ref, x)

    pl.semaphore_wait(barrier, peers - 1 + len(strides))

    def copy(src, dst, send, recv, device):
        return pltpu.make_async_remote_copy(
            src_ref=src, dst_ref=dst, send_sem=send, recv_sem=recv, device_id=device, device_id_type=MESH
        )

    halo = []
    for h, (dx, dy) in enumerate(HALO):
        first, count = {-1: (0, 1), 0: (0, 4), 1: (3, 1)}[dx]
        halo.append(
            copy(
                planes.at[pl.ds(first, count)], rim.at[h, pl.ds(0, count)],
                halo_s.at[h], halo_r.at[h], at_xy(dx, dy),
            )
        )
        halo[-1].start()
    for one in halo:
        one.wait_recv()

    inside_x = {-1: ix < nx - 1, 0: None, 1: ix > 0}
    inside_y = {-1: iy < ny - 1, 0: None, 1: iy > 0}

    def guarded(value, dx, dy):
        for ok in (inside_x[dx], inside_y[dy]):
            if ok is not None:
                value = jnp.where(ok, value, 0.0)
        return value

    def beside(plane, dy):
        if plane == 0 or plane == 5:
            dx = -1 if plane == 0 else 1
            return guarded(rim[HALO.index((-dx, -dy)), 0], -dx, -dy)
        if dy == 0:
            return planes[plane - 1]
        return guarded(rim[HALO.index((0, -dy)), plane - 1], 0, -dy)

    shifted = {}
    for plane in range(6):
        centre = beside(plane, 0)
        below = jnp.where(lane < 32, pltpu.roll(beside(plane, -1), 32, 1), pltpu.roll(centre, 32, 1))
        above = jnp.where(lane >= 96, pltpu.roll(beside(plane, 1), 96, 1), pltpu.roll(centre, 96, 1))
        for b, value in enumerate((below, centre, above)):
            shifted[plane, b, 0] = jnp.where(depth > 0, pltpu.roll(value, 1, 1), 0.0)
            shifted[plane, b, 1] = value
            shifted[plane, b, 2] = jnp.where(depth < 31, pltpu.roll(value, 127, 1), 0.0)
    rows = []
    for a in range(3):
        for b in range(3):
            for c in range(3):
                rows.append(jnp.concatenate([shifted[x + a, b, c] for x in range(4)], axis=1))
    ones = jnp.where(lax.broadcasted_iota(jnp.int32, (8, 512), 0) == 0, 1.0, 0.0)
    patches = jnp.concatenate(rows + [ones], axis=0).astype(BF16)
    weight = jnp.concatenate([w_ref[...].astype(F32), jnp.zeros((8, chans), F32)], axis=0).astype(BF16)

    partial = lax.dot_general(weight, patches, (((0,), (0,)), ((), ())), preferred_element_type=F32)

    def folded(block):
        return jnp.concatenate([block[:, :256], block[:, 256:]], axis=0)

    for owner in range(nz):
        block = partial[owner * 8 : owner * 8 + 8]
        part[owner % CLASSES, owner // CLASSES] = folded(block).astype(BF16)

    c1, c2, c3 = (lax.rem(cls + s, CLASSES) for s in (1, 2, 3))
    low, high = pl.ds(0, half), pl.ds(half, groups - half)
    stage = [
        copy(part.at[c1], near.at[0], rs1_s.at[0], rs1_r.at[0], at_z(1)),
        copy(part.at[c3], near.at[1], rs1_s.at[1], rs1_r.at[1], at_z(-1)),
        copy(part.at[c2, low], near.at[2, low], rs1_s.at[2], rs1_r.at[2], at_z(2)),
        copy(part.at[c2, high], near.at[2, high], rs1_s.at[3], rs1_r.at[3], at_z(-2)),
    ]
    for one in stage:
        one.start()
    for one in stage:
        one.wait_recv()
    sent = halo + stage
    acc[...] = (
        part[cls].astype(F32) + near[0].astype(F32) + near[1].astype(F32) + near[2].astype(F32)
    ).astype(BF16)

    stage = []
    for k in range(1, groups):
        stage.append(
            copy(
                acc.at[lax.rem(grp + k, groups)], far.at[k - 1],
                rs2_s.at[k - 1], rs2_r.at[k - 1], at_z(CLASSES * k),
            )
        )
        stage[-1].start()
    for one in stage:
        one.wait_recv()
    sent += stage
    pre = acc[grp].astype(F32)
    for k in range(groups - 1):
        pre = pre + far[k].astype(F32)

    square = lax.broadcasted_iota(jnp.int32, (8, 8), 0) == lax.broadcasted_iota(jnp.int32, (8, 8), 1)
    spread = jnp.broadcast_to(bias_ref[...].astype(F32), (8, 8))
    column = jnp.sum(jnp.where(square, spread, 0.0), axis=1, keepdims=True)
    pre = pre + jnp.concatenate([column, column], axis=0)
    sig = jax.nn.sigmoid(pre)
    cot = folded(jnp.concatenate([joined(cot_ref, x) for x in range(4)], axis=1))
    gath[cls, grp] = (cot * sig * (1.0 + pre * (1.0 - sig))).astype(BF16)

    stage = []
    for k in range(1, groups):
        stage.append(
            copy(
                gath.at[cls, grp], gath.at[cls, grp],
                ag1_s.at[k - 1], ag1_r.at[k - 1], at_z(CLASSES * k),
            )
        )
        stage[-1].start()

    act = (pre * sig).astype(BF16)
    for x in range(4):
        for y in range(4):
            first = (x % 2) * 128 + y * 32
            act_ref[x, y] = act[(x // 2) * 8 : (x // 2) * 8 + 8, first : first + 32]

    for one in stage:
        one.wait_recv()
    sent += stage
    stage = [
        copy(gath.at[cls], gath.at[cls], ag2_s.at[0], ag2_r.at[0], at_z(1)),
        copy(gath.at[cls], gath.at[cls], ag2_s.at[1], ag2_r.at[1], at_z(-1)),
        copy(gath.at[cls, low], gath.at[cls, low], ag2_s.at[2], ag2_r.at[2], at_z(2)),
        copy(gath.at[cls, high], gath.at[cls, high], ag2_s.at[3], ag2_r.at[3], at_z(-2)),
    ]
    for one in stage:
        one.start()
    for one in stage:
        one.wait_recv()
    sent += stage

    blocks = []
    for owner in range(nz):
        block = gath[owner % CLASSES, owner // CLASSES].astype(F32)
        blocks.append(jnp.concatenate([block[:8], block[8:]], axis=1))
    slope = jnp.concatenate(blocks, axis=0).astype(BF16)

    product = lax.dot_general(patches, slope, (((1,), (1,)), ((), ())), preferred_element_type=F32)
    size = 256 // peers
    for d in range(peers):
        top = min(max(224 - d * size, 0), size)
        if top:
            grad[d, :top] = product[d * size : d * size + top]
        if top < size:
            grad[d, top:] = jnp.zeros((size - top, chans), F32)

    me = ix * ny + iy

    def scatter(k):
        dx, dy = lax.div(k, ny), lax.rem(k, ny)
        gx, gy, gz = at_xy(dx, dy)
        return copy(grad.at[gx * ny + gy], pieces.at[k - 1], wr_s.at[k - 1], wr_r.at[k - 1], (gx, gy, gz))

    def spread_out(k):
        return copy(
            total.at[me], total.at[me], wa_s.at[k - 1], wa_r.at[k - 1],
            at_xy(lax.div(k, ny), lax.rem(k, ny)),
        )

    @pl.loop(1, peers)
    def _(k):
        scatter(k).start()

    taps = jnp.dot(weight, slope, preferred_element_type=F32)

    def tap_rows(a, b, c, x):
        first = ((a * 3 + b) * 3 + c) * 8
        return taps[first : first + 8, x * 128 : x * 128 + 128]

    own = {}
    for plane in range(6):
        moved = []
        for b in range(3):
            by_depth = []
            for c in range(3):
                terms = [tap_rows(a, b, c, plane - a) for a in range(3) if 0 <= plane - a < 4]
                by_depth.append(functools.reduce(jnp.add, terms))
            moved.append(
                by_depth[1]
                + jnp.where(depth < 31, pltpu.roll(by_depth[0], 127, 1), 0.0)
                + jnp.where(depth > 0, pltpu.roll(by_depth[2], 1, 1), 0.0)
            )
        down, up = pltpu.roll(moved[0], 96, 1), pltpu.roll(moved[2], 32, 1)
        own[plane, 0] = moved[1] + jnp.where(lane < 96, down, 0.0) + jnp.where(lane >= 32, up, 0.0)
        own[plane, -1] = jnp.where(lane >= 96, down, 0.0)
        own[plane, 1] = jnp.where(lane < 32, up, 0.0)

    moves = []
    for h, (dx, dy) in enumerate(HALO):
        if dx == 0:
            for x in range(4):
                back[h, x] = own[x + 1, dy]
        else:
            back[h, 0] = own[0 if dx < 0 else 5, dy]
        count = 4 if dx == 0 else 1
        moves.append(
            copy(
                back.at[h, pl.ds(0, count)], back_in.at[h, pl.ds(0, count)],
                bk_s.at[h], bk_r.at[h], at_xy(dx, dy),
            )
        )
        moves[-1].start()

    @pl.loop(1, peers)
    def _(k):
        scatter(k).wait_recv()

    whole = grad[me]
    for k in range(peers - 1):
        whole = whole + pieces[k]
    total[me] = whole * factor

    @pl.loop(1, peers)
    def _(k):
        spread_out(k).start()

    for one in moves:
        one.wait_recv()
    sums = [own[x + 1, 0] for x in range(4)]
    for h, (dx, dy) in enumerate(HALO):
        if dx == 0:
            for x in range(4):
                sums[x] = sums[x] + guarded(back_in[h, x], dx, dy)
        else:
            x = 3 if dx < 0 else 0
            sums[x] = sums[x] + guarded(back_in[h, 0], dx, dy)
    for x in range(4):
        plane = sums[x].astype(BF16)
        for y in range(4):
            ig_ref[x, y] = plane[:, y * 32 : y * 32 + 32]

    @pl.loop(1, peers)
    def _(k):
        spread_out(k).wait_recv()

    for d in range(peers):
        top = min(max(216 - d * size, 0), size)
        if top:
            wg_ref[d * size : d * size + top] = total[d, :top]
    line = total[216 // size, 216 % size : 216 % size + 1]
    line = jnp.broadcast_to(line, (8, chans))
    own_line = lax.broadcasted_iota(jnp.int32, (8, chans), 1) - iz * 8
    mine = own_line == lax.broadcasted_iota(jnp.int32, (8, chans), 0)
    bg_ref[...] = jnp.sum(jnp.where(mine, line, 0.0), axis=1, keepdims=True)

    for one in sent + moves:
        one.wait_send()

    @pl.loop(1, peers)
    def _(k):
        scatter(k).wait_send()
        spread_out(k).wait_send()


def body(nx, ny, nz, inputs, weight, bias, cotangent):
    groups = nz // CLASSES
    peers = nx * ny
    chans = 8 * nz
    size = 256 // peers
    factor = 1.0 / math.sqrt(512 * peers)
    vmem = pl.BlockSpec(memory_space=pltpu.VMEM)
    sems = [8, 8, 4, 4, groups - 1, groups - 1, groups - 1, groups - 1, 4, 4]
    sems += [peers - 1] * 4 + [8, 8]
    act, grad_in, grad_w, grad_b = pl.pallas_call(
        functools.partial(kernel, nx, ny, nz, factor),
        out_shape=(
            jax.ShapeDtypeStruct((4, 4, 8, 32), BF16),
            jax.ShapeDtypeStruct((4, 4, 8, 32), BF16),
            jax.ShapeDtypeStruct((216, chans), F32),
            jax.ShapeDtypeStruct((8, 1), F32),
        ),
        in_specs=[vmem] * 4,
        out_specs=(vmem,) * 4,
        scratch_shapes=[
            pltpu.VMEM((4, 8, 128), F32),
            pltpu.VMEM((8, 4, 8, 128), F32),
            pltpu.VMEM((CLASSES, groups, 16, 256), BF16),
            pltpu.VMEM((3, groups, 16, 256), BF16),
            pltpu.VMEM((groups, 16, 256), BF16),
            pltpu.VMEM((groups - 1, 16, 256), BF16),
            pltpu.VMEM((CLASSES, groups, 16, 256), BF16),
            pltpu.VMEM((peers, size, chans), F32),
            pltpu.VMEM((peers - 1, size, chans), F32),
            pltpu.VMEM((peers, size, chans), F32),
            pltpu.VMEM((8, 4, 8, 128), F32),
            pltpu.VMEM((8, 4, 8, 128), F32),
        ]
        + [pltpu.SemaphoreType.DMA((n,)) for n in sems],
        compiler_params=pltpu.CompilerParams(collective_id=0, has_side_effects=True),
    )(
        jnp.transpose(inputs, (0, 1, 3, 2)),
        weight.reshape(216, chans),
        bias.reshape(1, 8),
        jnp.transpose(cotangent, (0, 1, 3, 2)),
    )
    return (
        jnp.transpose(act, (0, 1, 3, 2)),
        jnp.transpose(grad_in, (0, 1, 3, 2)),
        grad_w.reshape(3, 3, 3, 8, chans),
        grad_b.reshape(8),
    )


def solution(mesh):
    sizes = (mesh.shape["gx"], mesh.shape["gy"], mesh.shape["ch"])
    return jax.shard_map(
        functools.partial(body, *sizes),
        mesh=mesh,
        in_specs=(
            P("gx", "gy", None, "ch"),
            P(None, None, None, "ch", None),
            P("ch"),
            P("gx", "gy", None, "ch"),
        ),
        out_specs=(
            P("gx", "gy", None, "ch"),
            P("gx", "gy", None, "ch"),
            P(None, None, None, "ch", None),
            P("ch"),
        ),
        check_vma=False,
    )
```

time: 501 us -> 96.4 us (0.19)
  waiting for transfers between devices: 282 us -> 0 us
  blocking collectives: 117 us -> 0 us
  Pallas kernels: 0 us -> 90.5 us
  starting transfers between devices: 55.6 us -> 0 us
  between operations: 14.7 us -> 0.65 us
  matrix products: 13.9 us -> 0 us
  local copies, waits for them, and re-layouts: 14.4 us -> 4.31 us
    psum x1 -> x0, waiting for transfers between devices: 166 us -> none  [body(): lax.psum((kernel_sum * factor, local_bias * factor), ('gx', 'gy'))]
    reduce_scatter x1 -> x0, waiting for transfers between devices: 109 us -> none  [body(): lax.psum_scatter(lax.dot_general(flat_weight, patches, (((0,), (1,)), (()...]
    pallas_call x0 -> x1, Pallas kernels: none -> 90.5 us  [body(): pl.pallas_call(functools.partial(kernel, nx, ny, nz, factor), out_shape=(...]
    psum x1 -> x0, blocking collectives: 61.3 us -> none  [body(): lax.psum((kernel_sum * factor, local_bias * factor), ('gx', 'gy'))]
    all_gather x1 -> x0, blocking collectives: 55.8 us -> none  [body(): piece = lax.all_gather(slope_rimmed, 'ch', axis=3, tiled=True)]
    ppermute x8 -> x0, starting transfers between devices: 55.5 us -> none  [the longest x4 40.3 us: with_halo(): before = lax.ppermute(last, axis, up)]
    dot_general x29 -> x0, matrix products: 13.9 us -> none  [the longest x27 12.7 us: body(): jnp.dot(cut, weight_turned[index], preferred_element_type=jnp.float32)]
    ppermute x8 -> x0, waiting for transfers between devices: 6.54 us -> none  [the longest x4 6.53 us: with_halo(): after = lax.ppermute(initial, axis, down)]
  transfers between devices with their start and end apart: 10 -> 0, of which waited for: 4 -> 0; matrix products, arithmetic and copies ran while one was open for 3% -> 0% of each run, Pallas kernels for 0% -> 0%
where the time goes in v1:
time: 96.4 us; the launch traced here: 96.1 us
  Pallas kernels  90.5 us (94%)
  local copies, waits for them, and re-layouts  4.31 us (4%)
    pallas_call x1, Pallas kernels, body(): pl.pallas_call(functools.partial(kernel, nx, ny, nz, factor), out_shape=(...  90.5 us
    unnamed x7, local copies, waits for them, and re-layouts  4.31 us

profile of v1, /device:TPU:1, one launch (start us, length us, event | category | flops | bytes accessed | tf_op | source)
XLA Modules:
  0.0 96.1 jit_solution(5612030818296238078)
XLA Ops:
  0.6 90.5 %shard_map.75 = (bf16[4,4,8,32]{3,2,1,0:T(8,128)(2,1)}, bf16[4,4,8,32]{3,2,1,0:T(8,128)(2,1)}, f32[216,256]{1,0:T(8,128)}, f32[8,1]{1,0:T(8,128)}) custom-call(bf16[4,4,8,32]{3,2,1,0:T(8,128)(2,1)} %bitcast.11, bf16[216,256]{1,0:T(8,128)(2,1)} %bitcast.8, bf16[1,8]{1,0:T(2,128)(2,1)} %bitcast.13, bf16[4,4,8,32]{3,2,1,0:T(8,128)(2,1)} %bitcast.12), custom_call_target="tpu_custom_call" | custom-call | tf_op jit(solution)/shard_map/pallas_call | solution.py:329
  91.2 0.0 copy-start.1
  91.2 0.7 copy-done.1
  91.9 0.6 reduce
  92.5 0.0 copy-start
  92.5 1.4 %copy.11 = bf16[4,4,32,8]{2,3,1,0:T(8,128)(2,1)} copy(bf16[4,4,32,8]{2,3,1,0:T(8,128)(2,1)} %bitcast.10) | data formatting | bytes 16384
  93.9 0.0 copy-done
  93.9 0.6 copy.12
  94.5 1.6 %copy.13 = f32[3,3,3,8,256]{4,3,2,1,0:T(8,128)} copy(f32[3,3,3,8,256]{4,3,2,1,0:T(8,128)} %bitcast.7) | data formatting | bytes 442368
Async XLA Ops:
  91.2 0.7 copy-start.1
  92.5 1.4 %copy-start = (bf16[4,4,8,32]{3,2,1,0:T(8,128)(2,1)S(1)}, bf16[4,4,8,32]{3,2,1,0:T(8,128)(2,1)}, u32[]{:S(2)}) copy-start(bf16[4,4,8,32]{3,2,1,0:T(8,128)(2,1)} %get-tuple-element.9) | copy-start | bytes 24580

commit v2 on v1

--- a/solution.py
+++ b/solution.py
@@ -17,10 +17,11 @@
 
 def kernel(
     nx, ny, nz, factor,
-    x_ref, w_ref, bias_ref, cot_ref,
-    act_ref, ig_ref, wg_ref, bg_ref,
-    planes, rim, part, near, acc, far, gath, grad, pieces, total, back, back_in,
-    halo_s, halo_r, rs1_s, rs1_r, rs2_s, rs2_r, ag1_s, ag1_r, ag2_s, ag2_r,
+    x_hbm, w_hbm, bias_ref, cot_hbm,
+    act_hbm, ig_hbm, wg_hbm, bg_ref,
+    x_ref, w_ref, cot_ref, act_ref, ig_ref, wg_ref,
+    planes, rim, part, near, acc, far, mine, gath, grad, pieces, total, back, back_in,
+    local, tokens, halo_s, halo_r, rs1_s, rs1_r, rs2_s, rs2_r, ag1_s, ag1_r, ag2_s, ag2_r,
     wr_s, wr_r, wa_s, wa_r, bk_s, bk_r,
 ):
     ix, iy, iz = lax.axis_index("gx"), lax.axis_index("gy"), lax.axis_index("ch")
@@ -29,6 +30,14 @@
     peers = nx * ny
     chans = 8 * nz
     cls, grp = lax.rem(iz, CLASSES), lax.div(iz, CLASSES)
+    held = lax.rem(cls + 2, CLASSES)
+
+    loads = [
+        pltpu.make_async_copy(src, dst, local.at[n])
+        for n, (src, dst) in enumerate(((x_hbm, x_ref), (w_hbm, w_ref), (cot_hbm, cot_ref)))
+    ]
+    for one in loads:
+        one.start()
 
     def at_xy(dx, dy):
         return (lax.rem(ix + dx + nx, nx), lax.rem(iy + dy + ny, ny), iz)
@@ -41,24 +50,34 @@
     def greet(device):
         pl.semaphore_signal(barrier, inc=1, device_id=device, device_id_type=MESH)
 
-    @pl.loop(1, peers)
-    def _(k):
-        greet(at_xy(lax.div(k, ny), lax.rem(k, ny)))
-
-    strides = [1, nz - 1, 2, nz - 2] + [CLASSES * k for k in range(1, groups)]
+    strides = [1, -1, 2, -2, 4, -4]
     for dz in strides:
         greet(at_z(dz))
 
+    @pl.loop(1, peers)
+    def _(k):
+        greet(at_xy(lax.div(k, ny), lax.rem(k, ny)))
+
     lane = lax.broadcasted_iota(jnp.int32, (8, 128), 1)
     depth = lax.rem(lane, 32)
 
     def joined(ref, x):
         return jnp.concatenate([ref[x, y].astype(F32) for y in range(4)], axis=1)
 
+    loads[0].wait()
     for x in range(4):
         planes[x] = joined(x_ref, x)
 
     pl.semaphore_wait(barrier, peers - 1 + len(strides))
+
+    rounds = half - 1
+
+    def pass_tokens():
+        for side, dz in enumerate((4, -4)):
+            pl.semaphore_signal(tokens.at[side], inc=1, device_id=at_z(dz), device_id_type=MESH)
+
+    if rounds:
+        pass_tokens()
 
     def copy(src, dst, send, recv, device):
         return pltpu.make_async_remote_copy(
@@ -75,6 +94,8 @@
             )
         )
         halo[-1].start()
+    loads[1].wait()
+    weight = jnp.concatenate([w_ref[...].astype(F32), jnp.zeros((8, chans), F32)], axis=0).astype(BF16)
     for one in halo:
         one.wait_recv()
 
@@ -111,88 +132,99 @@
                 rows.append(jnp.concatenate([shifted[x + a, b, c] for x in range(4)], axis=1))
     ones = jnp.where(lax.broadcasted_iota(jnp.int32, (8, 512), 0) == 0, 1.0, 0.0)
     patches = jnp.concatenate(rows + [ones], axis=0).astype(BF16)
-    weight = jnp.concatenate([w_ref[...].astype(F32), jnp.zeros((8, chans), F32)], axis=0).astype(BF16)
 
     partial = lax.dot_general(weight, patches, (((0,), (0,)), ((), ())), preferred_element_type=F32)
 
     def folded(block):
-        return jnp.concatenate([block[:, :256], block[:, 256:]], axis=0)
+        width = block.shape[1] // 2
+        return jnp.concatenate([block[:, :width], block[:, width:]], axis=0)
 
     for owner in range(nz):
         block = partial[owner * 8 : owner * 8 + 8]
         part[owner % CLASSES, owner // CLASSES] = folded(block).astype(BF16)
 
-    c1, c2, c3 = (lax.rem(cls + s, CLASSES) for s in (1, 2, 3))
-    low, high = pl.ds(0, half), pl.ds(half, groups - half)
-    stage = [
-        copy(part.at[c1], near.at[0], rs1_s.at[0], rs1_r.at[0], at_z(1)),
-        copy(part.at[c3], near.at[1], rs1_s.at[1], rs1_r.at[1], at_z(-1)),
-        copy(part.at[c2, low], near.at[2, low], rs1_s.at[2], rs1_r.at[2], at_z(2)),
-        copy(part.at[c2, high], near.at[2, high], rs1_s.at[3], rs1_r.at[3], at_z(-2)),
-    ]
-    for one in stage:
-        one.start()
-    for one in stage:
-        one.wait_recv()
-    sent = halo + stage
-    acc[...] = (
-        part[cls].astype(F32) + near[0].astype(F32) + near[1].astype(F32) + near[2].astype(F32)
-    ).astype(BF16)
-
-    stage = []
-    for k in range(1, groups):
-        stage.append(
-            copy(
-                acc.at[lax.rem(grp + k, groups)], far.at[k - 1],
-                rs2_s.at[k - 1], rs2_r.at[k - 1], at_z(CLASSES * k),
+    order = sorted(range(-half, half), key=lambda j: -abs(4 * j + 2))
+    batches = [order[:half], order[half:]] if half > 1 else [order]
+    sources = [(1, None), (-1, None), (2, range(0, half)), (-2, range(1 - half, 1))]
+
+    def owner_group(device, j):
+        return lax.div(lax.rem(iz + device + 4 * j + 2 + nz, nz), CLASSES)
+
+    near_sent = []
+    for n, batch in enumerate(batches):
+        for j in batch:
+            for s, (dz, members) in enumerate(sources):
+                if members is None or j in members:
+                    kind = lax.rem(cls + dz + 2 + CLASSES, CLASSES)
+                    one = copy(
+                        part.at[kind, owner_group(dz, j)], near.at[s, j + half],
+                        rs1_s.at[s, n], rs1_r.at[s, n], at_z(dz),
+                    )
+                    one.start()
+                    near_sent.append(one)
+
+    for r in range(rounds):
+        for side in range(2):
+            pl.semaphore_wait(tokens.at[side], 1)
+        if r < rounds - 1:
+            pass_tokens()
+
+    sent = list(halo)
+    counts = {}
+    for n, batch in enumerate(batches):
+        for s, (dz, members) in enumerate(sources):
+            counts[s, n] = len([j for j in batch if members is None or j in members])
+            if counts[s, n]:
+                span = near.at[s, pl.ds(0, counts[s, n])]
+                copy(span, span, rs1_s.at[s, n], rs1_r.at[s, n], at_z(dz)).wait_recv()
+        for j in batch:
+            value = part[held, owner_group(0, j)].astype(F32)
+            for s, (dz, members) in enumerate(sources):
+                if members is None or j in members:
+                    value = value + near[s, j + half].astype(F32)
+            acc[j + half] = value.astype(BF16)
+            one = copy(
+                acc.at[j + half], far.at[j + half], rs2_s.at[j + half], rs2_r.at[j + half], at_z(4 * j + 2)
             )
-        )
-        stage[-1].start()
-    for one in stage:
-        one.wait_recv()
-    sent += stage
-    pre = acc[grp].astype(F32)
-    for k in range(groups - 1):
-        pre = pre + far[k].astype(F32)
+            one.start()
+            sent.append(one)
 
     square = lax.broadcasted_iota(jnp.int32, (8, 8), 0) == lax.broadcasted_iota(jnp.int32, (8, 8), 1)
     spread = jnp.broadcast_to(bias_ref[...].astype(F32), (8, 8))
     column = jnp.sum(jnp.where(square, spread, 0.0), axis=1, keepdims=True)
-    pre = pre + jnp.concatenate([column, column], axis=0)
+    pre = jnp.concatenate([column, column], axis=0)
+    loads[2].wait()
+    cot = folded(jnp.concatenate([joined(cot_ref, x) for x in range(4)], axis=1))
+    for j in reversed(order):
+        copy(
+            acc.at[j + half], far.at[j + half], rs2_s.at[j + half], rs2_r.at[j + half], at_z(4 * j + 2)
+        ).wait_recv()
+        pre = pre + far[j + half].astype(F32)
     sig = jax.nn.sigmoid(pre)
-    cot = folded(jnp.concatenate([joined(cot_ref, x) for x in range(4)], axis=1))
-    gath[cls, grp] = (cot * sig * (1.0 + pre * (1.0 - sig))).astype(BF16)
-
-    stage = []
-    for k in range(1, groups):
-        stage.append(
-            copy(
-                gath.at[cls, grp], gath.at[cls, grp],
-                ag1_s.at[k - 1], ag1_r.at[k - 1], at_z(CLASSES * k),
-            )
-        )
-        stage[-1].start()
+    mine[...] = (cot * sig * (1.0 + pre * (1.0 - sig))).astype(BF16)
+
+    for j in order:
+        one = copy(mine, gath.at[cls, grp], ag1_s.at[j + half], ag1_r.at[j + half], at_z(4 * j + 2))
+        one.start()
+        sent.append(one)
 
     act = (pre * sig).astype(BF16)
     for x in range(4):
         for y in range(4):
             first = (x % 2) * 128 + y * 32
             act_ref[x, y] = act[(x // 2) * 8 : (x // 2) * 8 + 8, first : first + 32]
-
-    for one in stage:
-        one.wait_recv()
-    sent += stage
-    stage = [
-        copy(gath.at[cls], gath.at[cls], ag2_s.at[0], ag2_r.at[0], at_z(1)),
-        copy(gath.at[cls], gath.at[cls], ag2_s.at[1], ag2_r.at[1], at_z(-1)),
-        copy(gath.at[cls, low], gath.at[cls, low], ag2_s.at[2], ag2_r.at[2], at_z(2)),
-        copy(gath.at[cls, high], gath.at[cls, high], ag2_s.at[3], ag2_r.at[3], at_z(-2)),
-    ]
-    for one in stage:
-        one.start()
-    for one in stage:
-        one.wait_recv()
-    sent += stage
+    stores = [pltpu.make_async_copy(act_ref, act_hbm, local.at[3])]
+    stores[0].start()
+
+    for j in reversed(order):
+        slot = gath.at[held, owner_group(0, -j - 1)]
+        copy(mine, slot, ag1_s.at[j + half], ag1_r.at[j + half], at_z(4 * j + 2)).wait_recv()
+        for s, (dz, members) in enumerate(sources):
+            if members is None or j in members:
+                copy(slot, slot, ag2_s.at[s], ag2_r.at[s], at_z(dz)).start()
+    for s, (dz, members) in enumerate(sources):
+        span = gath.at[0] if members is None else gath.at[0, pl.ds(0, half)]
+        copy(span, span, ag2_s.at[s], ag2_r.at[s], at_z(dz)).wait_recv()
 
     blocks = []
     for owner in range(nz):
@@ -204,16 +236,15 @@
     size = 256 // peers
     for d in range(peers):
         top = min(max(224 - d * size, 0), size)
-        if top:
-            grad[d, :top] = product[d * size : d * size + top]
+        lines = [product[d * size : d * size + top]] if top else []
         if top < size:
-            grad[d, top:] = jnp.zeros((size - top, chans), F32)
+            lines.append(jnp.zeros((size - top, chans), F32))
+        grad[d] = folded(jnp.concatenate(lines, axis=0)).astype(BF16)
 
     me = ix * ny + iy
 
     def scatter(k):
-        dx, dy = lax.div(k, ny), lax.rem(k, ny)
-        gx, gy, gz = at_xy(dx, dy)
+        gx, gy, gz = at_xy(lax.div(k, ny), lax.rem(k, ny))
         return copy(grad.at[gx * ny + gy], pieces.at[k - 1], wr_s.at[k - 1], wr_r.at[k - 1], (gx, gy, gz))
 
     def spread_out(k):
@@ -270,10 +301,10 @@
     def _(k):
         scatter(k).wait_recv()
 
-    whole = grad[me]
+    whole = grad[me].astype(F32)
     for k in range(peers - 1):
-        whole = whole + pieces[k]
-    total[me] = whole * factor
+        whole = whole + pieces[k].astype(F32)
+    total[me] = (whole * factor).astype(BF16)
 
     @pl.loop(1, peers)
     def _(k):
@@ -293,64 +324,103 @@
         plane = sums[x].astype(BF16)
         for y in range(4):
             ig_ref[x, y] = plane[:, y * 32 : y * 32 + 32]
+    stores.append(pltpu.make_async_copy(ig_ref, ig_hbm, local.at[4]))
+    stores[1].start()
+
+    for one in sent + moves:
+        one.wait_send()
+    for (s, n), count in counts.items():
+        if count:
+            span = near.at[s, pl.ds(0, count)]
+            copy(span, span, rs1_s.at[s, n], rs1_r.at[s, n], at_z(1)).wait_send()
+    for s, (dz, members) in enumerate(sources):
+        span = gath.at[0] if members is None else gath.at[0, pl.ds(0, half)]
+        copy(span, span, ag2_s.at[s], ag2_r.at[s], at_z(dz)).wait_send()
+
+    @pl.loop(1, peers)
+    def _(k):
+        scatter(k).wait_send()
 
     @pl.loop(1, peers)
     def _(k):
         spread_out(k).wait_recv()
+
+    def chunk(d):
+        value = total[d].astype(F32)
+        return jnp.concatenate([value[:size], value[size:]], axis=1)
 
     for d in range(peers):
         top = min(max(216 - d * size, 0), size)
         if top:
-            wg_ref[d * size : d * size + top] = total[d, :top]
-    line = total[216 // size, 216 % size : 216 % size + 1]
+            wg_ref[d * size : d * size + top] = chunk(d)[:top]
+    stores.append(pltpu.make_async_copy(wg_ref, wg_hbm, local.at[5]))
+    stores[2].start()
+    line = chunk(216 // size)[216 % size : 216 % size + 1]
     line = jnp.broadcast_to(line, (8, chans))
     own_line = lax.broadcasted_iota(jnp.int32, (8, chans), 1) - iz * 8
-    mine = own_line == lax.broadcasted_iota(jnp.int32, (8, chans), 0)
-    bg_ref[...] = jnp.sum(jnp.where(mine, line, 0.0), axis=1, keepdims=True)
-
-    for one in sent + moves:
-        one.wait_send()
-
-    @pl.loop(1, peers)
-    def _(k):
-        scatter(k).wait_send()
+    mine_line = own_line == lax.broadcasted_iota(jnp.int32, (8, chans), 0)
+    column = jnp.sum(jnp.where(mine_line, line, 0.0), axis=1, keepdims=True)
+    bg_ref[...] = jnp.sum(jnp.where(square, jnp.broadcast_to(column, (8, 8)), 0.0), axis=0, keepdims=True)
+
+    @pl.loop(1, peers)
+    def _(k):
         spread_out(k).wait_send()
+
+    for one in stores:
+        one.wait()
+
+
+def hand_on(*refs):
+    for source, target in zip(refs[:4], refs[4:]):
+        target[...] = source[...]
 
 
 def body(nx, ny, nz, inputs, weight, bias, cotangent):
     groups = nz // CLASSES
+    half = groups // 2
     peers = nx * ny
     chans = 8 * nz
     size = 256 // peers
     factor = 1.0 / math.sqrt(512 * peers)
     vmem = pl.BlockSpec(memory_space=pltpu.VMEM)
-    sems = [8, 8, 4, 4, groups - 1, groups - 1, groups - 1, groups - 1, 4, 4]
-    sems += [peers - 1] * 4 + [8, 8]
-    act, grad_in, grad_w, grad_b = pl.pallas_call(
+    hbm = pl.BlockSpec(memory_space=pl.ANY)
+    sems = [(6,)] + [(8,)] * 2 + [(4, 2)] * 2 + [(groups,)] * 4 + [(4,)] * 2 + [(peers - 1,)] * 4 + [(8,)] * 2
+    sems = [pltpu.SemaphoreType.DMA(n) for n in sems]
+    shapes = (
+        jax.ShapeDtypeStruct((4, 4, 8, 32), BF16),
+        jax.ShapeDtypeStruct((4, 4, 8, 32), BF16),
+        jax.ShapeDtypeStruct((216, chans), F32),
+        jax.ShapeDtypeStruct((1, 8), F32),
+    )
+    results = pl.pallas_call(
         functools.partial(kernel, nx, ny, nz, factor),
-        out_shape=(
-            jax.ShapeDtypeStruct((4, 4, 8, 32), BF16),
-            jax.ShapeDtypeStruct((4, 4, 8, 32), BF16),
-            jax.ShapeDtypeStruct((216, chans), F32),
-            jax.ShapeDtypeStruct((8, 1), F32),
-        ),
-        in_specs=[vmem] * 4,
-        out_specs=(vmem,) * 4,
+        out_shape=shapes,
+        in_specs=[hbm, hbm, vmem, hbm],
+        out_specs=(hbm, hbm, hbm, vmem),
         scratch_shapes=[
+            pltpu.VMEM((4, 4, 8, 32), BF16),
+            pltpu.VMEM((216, chans), BF16),
+            pltpu.VMEM((4, 4, 8, 32), BF16),
+            pltpu.VMEM((4, 4, 8, 32), BF16),
+            pltpu.VMEM((4, 4, 8, 32), BF16),
+            pltpu.VMEM((216, chans), F32),
             pltpu.VMEM((4, 8, 128), F32),
             pltpu.VMEM((8, 4, 8, 128), F32),
             pltpu.VMEM((CLASSES, groups, 16, 256), BF16),
-            pltpu.VMEM((3, groups, 16, 256), BF16),
+            pltpu.VMEM((4, groups, 16, 256), BF16),
             pltpu.VMEM((groups, 16, 256), BF16),
-            pltpu.VMEM((groups - 1, 16, 256), BF16),
+            pltpu.VMEM((groups, 16, 256), BF16),
+            pltpu.VMEM((16, 256), BF16),
             pltpu.VMEM((CLASSES, groups, 16, 256), BF16),
-            pltpu.VMEM((peers, size, chans), F32),
-            pltpu.VMEM((peers - 1, size, chans), F32),
-            pltpu.VMEM((peers, size, chans), F32),
+            pltpu.VMEM((peers, 2 * size, chans // 2), BF16),
+            pltpu.VMEM((peers - 1, 2 * size, chans // 2), BF16),
+            pltpu.VMEM((peers, 2 * size, chans // 2), BF16),
             pltpu.VMEM((8, 4, 8, 128), F32),
             pltpu.VMEM((8, 4, 8, 128), F32),
+            sems[0],
+            pltpu.SemaphoreType.REGULAR((2,)),
         ]
-        + [pltpu.SemaphoreType.DMA((n,)) for n in sems],
+        + sems[1:],
         compiler_params=pltpu.CompilerParams(collective_id=0, has_side_effects=True),
     )(
         jnp.transpose(inputs, (0, 1, 3, 2)),
@@ -358,6 +428,12 @@
         bias.reshape(1, 8),
         jnp.transpose(cotangent, (0, 1, 3, 2)),
     )
+    act, grad_in, grad_w, grad_b = pl.pallas_call(
+        hand_on,
+        out_shape=shapes,
+        in_specs=[vmem] * 4,
+        out_specs=(vmem,) * 4,
+    )(*results)
     return (
         jnp.transpose(act, (0, 1, 3, 2)),
         jnp.transpose(grad_in, (0, 1, 3, 2)),

time: 96.4 us -> 76.9 us (0.80)
  Pallas kernels: 90.5 us -> 76.1 us
  local copies, waits for them, and re-layouts: 4.31 us -> 0 us
    pallas_call x1 -> x2, Pallas kernels: 90.5 us -> 76.1 us  [the longest x1 74.4 us: body(): pl.pallas_call(functools.partial(kernel, nx, ny, nz, factor), out_shape=s...]
    unnamed x7 -> x0, local copies, waits for them, and re-layouts: 4.31 us -> none
where the time goes in v2:
time: 76.9 us; the launch traced here: 76.7 us
  Pallas kernels  76.1 us (99%)
    pallas_call x1, Pallas kernels, body(): pl.pallas_call(functools.partial(kernel, nx, ny, nz, factor), out_shape=s...  74.4 us
    pallas_call x1, Pallas kernels, body(): pl.pallas_call(hand_on, out_shape=shapes, in_specs=[vmem] * 4, out_specs=...  1.7 us

profile of v2, /device:TPU:1, one launch (start us, length us, event | category | flops | bytes accessed | tf_op | source)
XLA Modules:
  0.0 76.7 jit_solution(18177782577592009080)
XLA Ops:
  0.6 74.4 %shard_map.75 = (bf16[4,4,8,32]{3,2,1,0:T(8,128)(2,1)}, bf16[4,4,8,32]{3,2,1,0:T(8,128)(2,1)}, f32[216,256]{1,0:T(8,128)}, f32[1,8]{1,0:T(1,128)}) custom-call(bf16[4,4,8,32]{3,2,1,0:T(8,128)(2,1)} %bitcast.9, bf16[216,256]{1,0:T(8,128)(2,1)} %bitcast.8, bf16[1,8]{1,0:T(2,128)(2,1)} %bitcast.11, bf16[4,4,8,32]{3,2,1,0:T(8,128)(2,1)} %bitcast.10), custom_call_target="tpu_custom_call" | custom-call | tf_op jit(solution)/shard_map/pallas_call | solution.py:395
  75.0 1.7 %shard_map.76 = (bf16[4,4,8,32]{3,2,1,0:T(8,128)(2,1)}, bf16[4,4,8,32]{3,2,1,0:T(8,128)(2,1)}, f32[216,256]{1,0:T(8,128)}, f32[1,8]{1,0:T(1,128)}) custom-call(bf16[4,4,8,32]{3,2,1,0:T(8,128)(2,1)} %get-tuple-element.12.refs_0_, bf16[4,4,8,32]{3,2,1,0:T(8,128)(2,1)} %get-tuple-element.13.refs_1_, f32[216,256]{1,0:T(8,128)} %get-tuple-element.14.refs_2_, ...), custom_call_target="tpu_custom_call" | custom-call | tf_op jit(solution)/shard_map/pallas_call | solution.py:431

commit v3 on v2

--- a/solution.py
+++ b/solution.py
@@ -17,16 +17,17 @@
 
 def kernel(
     nx, ny, nz, factor,
-    x_hbm, w_hbm, bias_ref, cot_hbm,
-    act_hbm, ig_hbm, wg_hbm, bg_ref,
-    x_ref, w_ref, cot_ref, act_ref, ig_ref, wg_ref,
-    planes, rim, part, near, acc, far, mine, gath, grad, pieces, total, back, back_in,
-    local, tokens, halo_s, halo_r, rs1_s, rs1_r, rs2_s, rs2_r, ag1_s, ag1_r, ag2_s, ag2_r,
+    x_hbm, w_hbm, bias_hbm, cot_hbm,
+    act_hbm, ig_hbm, total,
+    x_ref, w_ref, bias_ref, cot_ref, act_ref, ig_ref,
+    planes, rim, part, near, acc, relay, far, mine, gath, grad, pieces, chunk, back, back_in,
+    local, tokens, halo_s, halo_r, rs1_s, rs1_r, rl_s, rl_r, rs2_s, rs2_r, ag1_s, ag1_r, ag2_s, ag2_r,
     wr_s, wr_r, wa_s, wa_r, bk_s, bk_r,
 ):
     ix, iy, iz = lax.axis_index("gx"), lax.axis_index("gy"), lax.axis_index("ch")
     groups = nz // CLASSES
     half = groups // 2
+    quarter = half // 2
     peers = nx * ny
     chans = 8 * nz
     cls, grp = lax.rem(iz, CLASSES), lax.div(iz, CLASSES)
@@ -34,7 +35,7 @@
 
     loads = [
         pltpu.make_async_copy(src, dst, local.at[n])
-        for n, (src, dst) in enumerate(((x_hbm, x_ref), (w_hbm, w_ref), (cot_hbm, cot_ref)))
+        for n, (src, dst) in enumerate(((x_hbm, x_ref), (w_hbm, w_ref), (cot_hbm, cot_ref), (bias_hbm, bias_ref)))
     ]
     for one in loads:
         one.start()
@@ -50,13 +51,10 @@
     def greet(device):
         pl.semaphore_signal(barrier, inc=1, device_id=device, device_id_type=MESH)
 
-    strides = [1, -1, 2, -2, 4, -4]
-    for dz in strides:
+    for dz in (1, -1, 2, -2):
         greet(at_z(dz))
-
-    @pl.loop(1, peers)
-    def _(k):
-        greet(at_xy(lax.div(k, ny), lax.rem(k, ny)))
+    for dx, dy in HALO:
+        greet(at_xy(dx, dy))
 
     lane = lax.broadcasted_iota(jnp.int32, (8, 128), 1)
     depth = lax.rem(lane, 32)
@@ -68,16 +66,18 @@
     for x in range(4):
         planes[x] = joined(x_ref, x)
 
-    pl.semaphore_wait(barrier, peers - 1 + len(strides))
-
-    rounds = half - 1
-
-    def pass_tokens():
-        for side, dz in enumerate((4, -4)):
-            pl.semaphore_signal(tokens.at[side], inc=1, device_id=at_z(dz), device_id_type=MESH)
-
-    if rounds:
-        pass_tokens()
+    pl.semaphore_wait(barrier, 4 + len(HALO))
+
+    def pass_token(n, device):
+        pl.semaphore_signal(tokens.at[n], inc=1, device_id=device, device_id_type=MESH)
+
+    def await_tokens(*ns):
+        for n in ns:
+            pl.semaphore_wait(tokens.at[n], 1)
+
+    if quarter:
+        pass_token(0, at_z(2))
+        pass_token(1, at_z(-2))
 
     def copy(src, dst, send, recv, device):
         return pltpu.make_async_remote_copy(
@@ -98,6 +98,13 @@
     weight = jnp.concatenate([w_ref[...].astype(F32), jnp.zeros((8, chans), F32)], axis=0).astype(BF16)
     for one in halo:
         one.wait_recv()
+    if ny > 4:
+        pass_token(4, at_xy(0, 2))
+        pass_token(5, at_xy(0, -2))
+    if quarter:
+        await_tokens(0, 1)
+        pass_token(2, at_z(4))
+        pass_token(3, at_z(-4))
 
     inside_x = {-1: ix < nx - 1, 0: None, 1: ix > 0}
     inside_y = {-1: iy < ny - 1, 0: None, 1: iy > 0}
@@ -144,7 +151,8 @@
         part[owner % CLASSES, owner // CLASSES] = folded(block).astype(BF16)
 
     order = sorted(range(-half, half), key=lambda j: -abs(4 * j + 2))
-    batches = [order[:half], order[half:]] if half > 1 else [order]
+    outer, inner = order[: 2 * quarter], order[2 * quarter :]
+    batches = [outer, inner]
     sources = [(1, None), (-1, None), (2, range(0, half)), (-2, range(1 - half, 1))]
 
     def owner_group(device, j):
@@ -163,14 +171,12 @@
                     one.start()
                     near_sent.append(one)
 
-    for r in range(rounds):
-        for side in range(2):
-            pl.semaphore_wait(tokens.at[side], 1)
-        if r < rounds - 1:
-            pass_tokens()
+    if quarter:
+        await_tokens(2, 3)
 
     sent = list(halo)
     counts = {}
+    relays = {}
     for n, batch in enumerate(batches):
         for s, (dz, members) in enumerate(sources):
             counts[s, n] = len([j for j in batch if members is None or j in members])
@@ -183,22 +189,32 @@
                 if members is None or j in members:
                     value = value + near[s, j + half].astype(F32)
             acc[j + half] = value.astype(BF16)
-            one = copy(
-                acc.at[j + half], far.at[j + half], rs2_s.at[j + half], rs2_r.at[j + half], at_z(4 * j + 2)
-            )
-            one.start()
-            sent.append(one)
+            if j in outer:
+                step = quarter if j > 0 else -quarter
+                slot = j - step + half
+                one = copy(acc.at[j + half], relay.at[slot], rl_s.at[slot], rl_r.at[slot], at_z(4 * step))
+                one.start()
+                relays[j - step] = one
+
+    far_in = []
+    for j in inner:
+        if quarter:
+            relays[j].wait()
+            acc[j + half] = (acc[j + half].astype(F32) + relay[j + half].astype(F32)).astype(BF16)
+        one = copy(acc.at[j + half], far.at[j + half], rs2_s.at[j + half], rs2_r.at[j + half], at_z(4 * j + 2))
+        one.start()
+        far_in.insert(0, (j, one))
+        sent.append(one)
 
     square = lax.broadcasted_iota(jnp.int32, (8, 8), 0) == lax.broadcasted_iota(jnp.int32, (8, 8), 1)
+    loads[3].wait()
     spread = jnp.broadcast_to(bias_ref[...].astype(F32), (8, 8))
     column = jnp.sum(jnp.where(square, spread, 0.0), axis=1, keepdims=True)
     pre = jnp.concatenate([column, column], axis=0)
     loads[2].wait()
     cot = folded(jnp.concatenate([joined(cot_ref, x) for x in range(4)], axis=1))
-    for j in reversed(order):
-        copy(
-            acc.at[j + half], far.at[j + half], rs2_s.at[j + half], rs2_r.at[j + half], at_z(4 * j + 2)
-        ).wait_recv()
+    for j, one in far_in:
+        one.wait_recv()
         pre = pre + far[j + half].astype(F32)
     sig = jax.nn.sigmoid(pre)
     mine[...] = (cot * sig * (1.0 + pre * (1.0 - sig))).astype(BF16)
@@ -243,19 +259,13 @@
 
     me = ix * ny + iy
 
-    def scatter(k):
-        gx, gy, gz = at_xy(lax.div(k, ny), lax.rem(k, ny))
-        return copy(grad.at[gx * ny + gy], pieces.at[k - 1], wr_s.at[k - 1], wr_r.at[k - 1], (gx, gy, gz))
-
-    def spread_out(k):
-        return copy(
-            total.at[me], total.at[me], wa_s.at[k - 1], wa_r.at[k - 1],
-            at_xy(lax.div(k, ny), lax.rem(k, ny)),
-        )
-
-    @pl.loop(1, peers)
-    def _(k):
-        scatter(k).start()
+    others = [(dx, dy) for dx in range(nx) for dy in range(ny) if (dx, dy) != (0, 0)]
+    others.sort(key=lambda d: -(min(d[0], nx - d[0]) + (min(d[1], ny - d[1]) + 1) // 2))
+    if ny > 4:
+        await_tokens(4, 5)
+    for n, (dx, dy) in enumerate(others):
+        gx, gy, gz = at_xy(dx, dy)
+        copy(grad.at[gx * ny + gy], pieces.at[n], wr_s, wr_r, (gx, gy, gz)).start()
 
     taps = jnp.dot(weight, slope, preferred_element_type=F32)
 
@@ -297,18 +307,15 @@
         )
         moves[-1].start()
 
-    @pl.loop(1, peers)
-    def _(k):
-        scatter(k).wait_recv()
-
+    copy(pieces, pieces, wr_s, wr_r, at_xy(0, 1)).wait_recv()
     whole = grad[me].astype(F32)
     for k in range(peers - 1):
         whole = whole + pieces[k].astype(F32)
-    total[me] = (whole * factor).astype(BF16)
-
-    @pl.loop(1, peers)
-    def _(k):
-        spread_out(k).start()
+    chunk[...] = (whole * factor).astype(BF16)
+    for dx, dy in others:
+        copy(chunk, total.at[me], wa_s, wa_r, at_xy(dx, dy)).start()
+    stores.append(pltpu.make_async_copy(chunk, total.at[me], local.at[5]))
+    stores[-1].start()
 
     for one in moves:
         one.wait_recv()
@@ -325,7 +332,7 @@
         for y in range(4):
             ig_ref[x, y] = plane[:, y * 32 : y * 32 + 32]
     stores.append(pltpu.make_async_copy(ig_ref, ig_hbm, local.at[4]))
-    stores[1].start()
+    stores[-1].start()
 
     for one in sent + moves:
         one.wait_send()
@@ -337,42 +344,32 @@
         span = gath.at[0] if members is None else gath.at[0, pl.ds(0, half)]
         copy(span, span, ag2_s.at[s], ag2_r.at[s], at_z(dz)).wait_send()
 
-    @pl.loop(1, peers)
-    def _(k):
-        scatter(k).wait_send()
-
-    @pl.loop(1, peers)
-    def _(k):
-        spread_out(k).wait_recv()
+    rest = total.at[pl.ds(0, peers - 1)]
+    copy(pieces, pieces, wr_s, wr_r, at_xy(0, 1)).wait_send()
+    copy(rest, rest, wa_s, wa_r, at_xy(0, 1)).wait()
+    for one in stores:
+        one.wait()
+
+
+def hand_on(size, act_in, ig_in, total, act, ig, wg, bg):
+    chans = wg.shape[1]
+    act[...] = act_in[...]
+    ig[...] = ig_in[...]
 
     def chunk(d):
         value = total[d].astype(F32)
         return jnp.concatenate([value[:size], value[size:]], axis=1)
 
-    for d in range(peers):
+    for d in range(total.shape[0]):
         top = min(max(216 - d * size, 0), size)
         if top:
-            wg_ref[d * size : d * size + top] = chunk(d)[:top]
-    stores.append(pltpu.make_async_copy(wg_ref, wg_hbm, local.at[5]))
-    stores[2].start()
-    line = chunk(216 // size)[216 % size : 216 % size + 1]
-    line = jnp.broadcast_to(line, (8, chans))
-    own_line = lax.broadcasted_iota(jnp.int32, (8, chans), 1) - iz * 8
-    mine_line = own_line == lax.broadcasted_iota(jnp.int32, (8, chans), 0)
-    column = jnp.sum(jnp.where(mine_line, line, 0.0), axis=1, keepdims=True)
-    bg_ref[...] = jnp.sum(jnp.where(square, jnp.broadcast_to(column, (8, 8)), 0.0), axis=0, keepdims=True)
-
-    @pl.loop(1, peers)
-    def _(k):
-        spread_out(k).wait_send()
-
-    for one in stores:
-        one.wait()
-
-
-def hand_on(*refs):
-    for source, target in zip(refs[:4], refs[4:]):
-        target[...] = source[...]
+            wg[d * size : d * size + top] = chunk(d)[:top]
+    line = jnp.broadcast_to(chunk(216 // size)[216 % size : 216 % size + 1], (8, chans))
+    lane = lax.broadcasted_iota(jnp.int32, (8, chans), 1) - lax.axis_index("ch") * 8
+    column = jnp.where(lane == lax.broadcasted_iota(jnp.int32, (8, chans), 0), line, 0.0)
+    column = jnp.broadcast_to(jnp.sum(column, axis=1, keepdims=True), (8, 8))
+    square = lax.broadcasted_iota(jnp.int32, (8, 8), 0) == lax.broadcasted_iota(jnp.int32, (8, 8), 1)
+    bg[...] = jnp.sum(jnp.where(square, column, 0.0), axis=0, keepdims=True)
 
 
 def body(nx, ny, nz, inputs, weight, bias, cotangent):
@@ -384,43 +381,39 @@
     factor = 1.0 / math.sqrt(512 * peers)
     vmem = pl.BlockSpec(memory_space=pltpu.VMEM)
     hbm = pl.BlockSpec(memory_space=pl.ANY)
-    sems = [(6,)] + [(8,)] * 2 + [(4, 2)] * 2 + [(groups,)] * 4 + [(4,)] * 2 + [(peers - 1,)] * 4 + [(8,)] * 2
-    sems = [pltpu.SemaphoreType.DMA(n) for n in sems]
-    shapes = (
-        jax.ShapeDtypeStruct((4, 4, 8, 32), BF16),
-        jax.ShapeDtypeStruct((4, 4, 8, 32), BF16),
-        jax.ShapeDtypeStruct((216, chans), F32),
-        jax.ShapeDtypeStruct((1, 8), F32),
-    )
+    sems = [(8,)] * 2 + [(4, 2)] * 2 + [(groups,)] * 6 + [(4,)] * 2 + [()] * 4 + [(8,)] * 2
+    cells = jax.ShapeDtypeStruct((4, 4, 8, 32), BF16)
+    gathered = jax.ShapeDtypeStruct((peers, 2 * size, chans // 2), BF16)
     results = pl.pallas_call(
         functools.partial(kernel, nx, ny, nz, factor),
-        out_shape=shapes,
-        in_specs=[hbm, hbm, vmem, hbm],
-        out_specs=(hbm, hbm, hbm, vmem),
+        out_shape=(cells, cells, gathered),
+        in_specs=[hbm] * 4,
+        out_specs=(hbm,) * 3,
         scratch_shapes=[
             pltpu.VMEM((4, 4, 8, 32), BF16),
             pltpu.VMEM((216, chans), BF16),
+            pltpu.VMEM((1, 8), BF16),
             pltpu.VMEM((4, 4, 8, 32), BF16),
             pltpu.VMEM((4, 4, 8, 32), BF16),
             pltpu.VMEM((4, 4, 8, 32), BF16),
-            pltpu.VMEM((216, chans), F32),
             pltpu.VMEM((4, 8, 128), F32),
             pltpu.VMEM((8, 4, 8, 128), F32),
             pltpu.VMEM((CLASSES, groups, 16, 256), BF16),
             pltpu.VMEM((4, groups, 16, 256), BF16),
             pltpu.VMEM((groups, 16, 256), BF16),
             pltpu.VMEM((groups, 16, 256), BF16),
+            pltpu.VMEM((groups, 16, 256), BF16),
             pltpu.VMEM((16, 256), BF16),
             pltpu.VMEM((CLASSES, groups, 16, 256), BF16),
             pltpu.VMEM((peers, 2 * size, chans // 2), BF16),
             pltpu.VMEM((peers - 1, 2 * size, chans // 2), BF16),
-            pltpu.VMEM((peers, 2 * size, chans // 2), BF16),
+            pltpu.VMEM((2 * size, chans // 2), BF16),
             pltpu.VMEM((8, 4, 8, 128), F32),
             pltpu.VMEM((8, 4, 8, 128), F32),
-            sems[0],
-            pltpu.SemaphoreType.REGULAR((2,)),
+            pltpu.SemaphoreType.DMA((6,)),
+            pltpu.SemaphoreType.REGULAR((6,)),
         ]
-        + sems[1:],
+        + [pltpu.SemaphoreType.DMA(n) for n in sems],
         compiler_params=pltpu.CompilerParams(collective_id=0, has_side_effects=True),
     )(
         jnp.transpose(inputs, (0, 1, 3, 2)),
@@ -429,9 +422,9 @@
         jnp.transpose(cotangent, (0, 1, 3, 2)),
     )
     act, grad_in, grad_w, grad_b = pl.pallas_call(
-        hand_on,
-        out_shape=shapes,
-        in_specs=[vmem] * 4,
+        functools.partial(hand_on, size),
+        out_shape=(cells, cells, jax.ShapeDtypeStruct((216, chans), F32), jax.ShapeDtypeStruct((1, 8), F32)),
+        in_specs=[vmem] * 3,
         out_specs=(vmem,) * 4,
     )(*results)
     return (

time: 76.9 us -> 73.2 us (0.952)
  Pallas kernels: 76.1 us -> 72.3 us
    pallas_call x2, Pallas kernels: 76.1 us -> 72.3 us  [the longest x1 70.7 us: body(): pl.pallas_call(functools.partial(kernel, nx, ny, nz, factor), out_shape=(...]
where the time goes in v3:
time: 73.2 us; the launch traced here: 73 us
  Pallas kernels  72.3 us (99%)
    pallas_call x1, Pallas kernels, body(): pl.pallas_call(functools.partial(kernel, nx, ny, nz, factor), out_shape=(...  70.7 us
    pallas_call x1, Pallas kernels, body(): pl.pallas_call(functools.partial(hand_on, size), out_shape=(cells, cells,...  1.66 us

profile of v3, /device:TPU:1, one launch (start us, length us, event | category | flops | bytes accessed | tf_op | source)
XLA Modules:
  0.0 73.0 jit_solution(3291579892296693781)
XLA Ops:
  0.6 70.7 %shard_map.75 = (bf16[4,4,8,32]{3,2,1,0:T(8,128)(2,1)}, bf16[4,4,8,32]{3,2,1,0:T(8,128)(2,1)}, bf16[32,16,128]{2,1,0:T(8,128)(2,1)}) custom-call(bf16[4,4,8,32]{3,2,1,0:T(8,128)(2,1)} %bitcast.9, bf16[216,256]{1,0:T(8,128)(2,1)} %bitcast.8, bf16[1,8]{1,0:T(2,128)(2,1)} %bitcast.11, bf16[4,4,8,32]{3,2,1,0:T(8,128)(2,1)} %bitcast.10), custom_call_target="tpu_custom_call" | custom-call | tf_op jit(solution)/shard_map/pallas_call | solution.py:387
  71.3 1.7 %shard_map.76 = (bf16[4,4,8,32]{3,2,1,0:T(8,128)(2,1)}, bf16[4,4,8,32]{3,2,1,0:T(8,128)(2,1)}, f32[216,256]{1,0:T(8,128)}, f32[1,8]{1,0:T(1,128)}) custom-call(bf16[4,4,8,32]{3,2,1,0:T(8,128)(2,1)} %get-tuple-element.11.act_in, bf16[4,4,8,32]{3,2,1,0:T(8,128)(2,1)} %get-tuple-element.12.ig_in, bf16[32,16,128]{2,1,0:T(8,128)(2,1)} %get-tuple-element.13.total), custom_call_target="tpu_custom_call" | custom-call | tf_op jit(solution)/shard_map/pallas_call | solution.py:424

commit v4 on v3

--- a/solution.py
+++ b/solution.py
@@ -20,8 +20,8 @@
     x_hbm, w_hbm, bias_hbm, cot_hbm,
     act_hbm, ig_hbm, total,
     x_ref, w_ref, bias_ref, cot_ref, act_ref, ig_ref,
-    planes, rim, part, near, acc, relay, far, mine, gath, grad, pieces, chunk, back, back_in,
-    local, tokens, halo_s, halo_r, rs1_s, rs1_r, rl_s, rl_r, rs2_s, rs2_r, ag1_s, ag1_r, ag2_s, ag2_r,
+    planes, rim, part, near, acc, far, mine, gath, grad, pieces, chunk, back, back_in,
+    local, tokens, halo_s, halo_r, rs1_s, rs1_r, rs2_s, rs2_r, ag1_s, ag1_r, ag2_s, ag2_r,
     wr_s, wr_r, wa_s, wa_r, bk_s, bk_r,
 ):
     ix, iy, iz = lax.axis_index("gx"), lax.axis_index("gy"), lax.axis_index("ch")
@@ -96,15 +96,19 @@
         halo[-1].start()
     loads[1].wait()
     weight = jnp.concatenate([w_ref[...].astype(F32), jnp.zeros((8, chans), F32)], axis=0).astype(BF16)
+    if quarter:
+        await_tokens(0, 1)
+        pass_token(2, at_z(4))
+        pass_token(3, at_z(-4))
     for one in halo:
         one.wait_recv()
     if ny > 4:
         pass_token(4, at_xy(0, 2))
         pass_token(5, at_xy(0, -2))
     if quarter:
-        await_tokens(0, 1)
-        pass_token(2, at_z(4))
-        pass_token(3, at_z(-4))
+        await_tokens(2, 3)
+        pass_token(6, at_z(8))
+        pass_token(7, at_z(-8))
 
     inside_x = {-1: ix < nx - 1, 0: None, 1: ix > 0}
     inside_y = {-1: iy < ny - 1, 0: None, 1: iy > 0}
@@ -146,65 +150,56 @@
         width = block.shape[1] // 2
         return jnp.concatenate([block[:, :width], block[:, width:]], axis=0)
 
+    turn = half + quarter
     for owner in range(nz):
+        way = lax.rem(owner - iz + nz, CLASSES)
+        apart = owner - iz - jnp.where(way == 0, CLASSES, way) + CLASSES * turn + nz
         block = partial[owner * 8 : owner * 8 + 8]
-        part[owner % CLASSES, owner // CLASSES] = folded(block).astype(BF16)
+        part[way, lax.rem(lax.div(apart, CLASSES), groups)] = folded(block).astype(BF16)
 
     order = sorted(range(-half, half), key=lambda j: -abs(4 * j + 2))
     outer, inner = order[: 2 * quarter], order[2 * quarter :]
     batches = [outer, inner]
     sources = [(1, None), (-1, None), (2, range(0, half)), (-2, range(1 - half, 1))]
 
+    def slot_of(j):
+        return (j + turn) % groups
+
     def owner_group(device, j):
         return lax.div(lax.rem(iz + device + 4 * j + 2 + nz, nz), CLASSES)
 
-    near_sent = []
+    stage = {}
     for n, batch in enumerate(batches):
+        for s, (dz, members) in enumerate(sources):
+            slots = sorted(slot_of(j) for j in batch if members is None or j in members)
+            if slots:
+                assert slots == list(range(slots[0], slots[0] + len(slots)))
+                stage[s, n] = copy(
+                    part.at[(3, 1, 0, 0)[s], pl.ds(slots[0] - (s == 3), len(slots))],
+                    near.at[s, pl.ds(slots[0], len(slots))],
+                    rs1_s.at[s, n], rs1_r.at[s, n], at_z(dz),
+                )
+                stage[s, n].start()
+
+    if quarter:
+        await_tokens(6, 7)
+
+    sent = list(halo)
+    far_in = []
+    for n, batch in enumerate(batches):
+        for s in range(4):
+            if (s, n) in stage:
+                stage[s, n].wait_recv()
         for j in batch:
+            value = part[2, slot_of(j)].astype(F32)
             for s, (dz, members) in enumerate(sources):
                 if members is None or j in members:
-                    kind = lax.rem(cls + dz + 2 + CLASSES, CLASSES)
-                    one = copy(
-                        part.at[kind, owner_group(dz, j)], near.at[s, j + half],
-                        rs1_s.at[s, n], rs1_r.at[s, n], at_z(dz),
-                    )
-                    one.start()
-                    near_sent.append(one)
-
-    if quarter:
-        await_tokens(2, 3)
-
-    sent = list(halo)
-    counts = {}
-    relays = {}
-    for n, batch in enumerate(batches):
-        for s, (dz, members) in enumerate(sources):
-            counts[s, n] = len([j for j in batch if members is None or j in members])
-            if counts[s, n]:
-                span = near.at[s, pl.ds(0, counts[s, n])]
-                copy(span, span, rs1_s.at[s, n], rs1_r.at[s, n], at_z(dz)).wait_recv()
-        for j in batch:
-            value = part[held, owner_group(0, j)].astype(F32)
-            for s, (dz, members) in enumerate(sources):
-                if members is None or j in members:
-                    value = value + near[s, j + half].astype(F32)
+                    value = value + near[s, slot_of(j)].astype(F32)
             acc[j + half] = value.astype(BF16)
-            if j in outer:
-                step = quarter if j > 0 else -quarter
-                slot = j - step + half
-                one = copy(acc.at[j + half], relay.at[slot], rl_s.at[slot], rl_r.at[slot], at_z(4 * step))
-                one.start()
-                relays[j - step] = one
-
-    far_in = []
-    for j in inner:
-        if quarter:
-            relays[j].wait()
-            acc[j + half] = (acc[j + half].astype(F32) + relay[j + half].astype(F32)).astype(BF16)
-        one = copy(acc.at[j + half], far.at[j + half], rs2_s.at[j + half], rs2_r.at[j + half], at_z(4 * j + 2))
-        one.start()
-        far_in.insert(0, (j, one))
-        sent.append(one)
+            one = copy(acc.at[j + half], far.at[j + half], rs2_s.at[j + half], rs2_r.at[j + half], at_z(4 * j + 2))
+            one.start()
+            far_in.insert(0, (j, one))
+            sent.append(one)
 
     square = lax.broadcasted_iota(jnp.int32, (8, 8), 0) == lax.broadcasted_iota(jnp.int32, (8, 8), 1)
     loads[3].wait()
@@ -336,10 +331,8 @@
 
     for one in sent + moves:
         one.wait_send()
-    for (s, n), count in counts.items():
-        if count:
-            span = near.at[s, pl.ds(0, count)]
-            copy(span, span, rs1_s.at[s, n], rs1_r.at[s, n], at_z(1)).wait_send()
+    for one in stage.values():
+        one.wait_send()
     for s, (dz, members) in enumerate(sources):
         span = gath.at[0] if members is None else gath.at[0, pl.ds(0, half)]
         copy(span, span, ag2_s.at[s], ag2_r.at[s], at_z(dz)).wait_send()
@@ -381,7 +374,7 @@
     factor = 1.0 / math.sqrt(512 * peers)
     vmem = pl.BlockSpec(memory_space=pltpu.VMEM)
     hbm = pl.BlockSpec(memory_space=pl.ANY)
-    sems = [(8,)] * 2 + [(4, 2)] * 2 + [(groups,)] * 6 + [(4,)] * 2 + [()] * 4 + [(8,)] * 2
+    sems = [(8,)] * 2 + [(4, 2)] * 2 + [(groups,)] * 4 + [(4,)] * 2 + [()] * 4 + [(8,)] * 2
     cells = jax.ShapeDtypeStruct((4, 4, 8, 32), BF16)
     gathered = jax.ShapeDtypeStruct((peers, 2 * size, chans // 2), BF16)
     results = pl.pallas_call(
@@ -402,7 +395,6 @@
             pltpu.VMEM((4, groups, 16, 256), BF16),
             pltpu.VMEM((groups, 16, 256), BF16),
             pltpu.VMEM((groups, 16, 256), BF16),
-            pltpu.VMEM((groups, 16, 256), BF16),
             pltpu.VMEM((16, 256), BF16),
             pltpu.VMEM((CLASSES, groups, 16, 256), BF16),
             pltpu.VMEM((peers, 2 * size, chans // 2), BF16),
@@ -411,7 +403,7 @@
             pltpu.VMEM((8, 4, 8, 128), F32),
             pltpu.VMEM((8, 4, 8, 128), F32),
             pltpu.SemaphoreType.DMA((6,)),
-            pltpu.SemaphoreType.REGULAR((6,)),
+            pltpu.SemaphoreType.REGULAR((8,)),
         ]
         + [pltpu.SemaphoreType.DMA(n) for n in sems],
         compiler_params=pltpu.CompilerParams(collective_id=0, has_side_effects=True),

time: 73.2 us -> 72.4 us (0.989)
    pallas_call x1, Pallas kernels: 70.7 us -> 69.9 us  [body(): pl.pallas_call(functools.partial(kernel, nx, ny, nz, factor), out_shape=(...]
where the time goes in v4:
time: 72.4 us; the launch traced here: 72.2 us
  Pallas kernels  71.6 us (99%)
    pallas_call x1, Pallas kernels, body(): pl.pallas_call(functools.partial(kernel, nx, ny, nz, factor), out_shape=(...  69.9 us
    pallas_call x1, Pallas kernels, body(): pl.pallas_call(functools.partial(hand_on, size), out_shape=(cells, cells,...  1.66 us

profile of v4, /device:TPU:1, one launch (start us, length us, event | category | flops | bytes accessed | tf_op | source)
XLA Modules:
  0.0 72.2 jit_solution(6935364137415152213)
XLA Ops:
  0.6 69.9 %shard_map.75 = (bf16[4,4,8,32]{3,2,1,0:T(8,128)(2,1)}, bf16[4,4,8,32]{3,2,1,0:T(8,128)(2,1)}, bf16[32,16,128]{2,1,0:T(8,128)(2,1)}) custom-call(bf16[4,4,8,32]{3,2,1,0:T(8,128)(2,1)} %bitcast.9, bf16[216,256]{1,0:T(8,128)(2,1)} %bitcast.8, bf16[1,8]{1,0:T(2,128)(2,1)} %bitcast.11, bf16[4,4,8,32]{3,2,1,0:T(8,128)(2,1)} %bitcast.10), custom_call_target="tpu_custom_call" | custom-call | tf_op jit(solution)/shard_map/pallas_call | solution.py:380
  70.5 1.7 %shard_map.76 = (bf16[4,4,8,32]{3,2,1,0:T(8,128)(2,1)}, bf16[4,4,8,32]{3,2,1,0:T(8,128)(2,1)}, f32[216,256]{1,0:T(8,128)}, f32[1,8]{1,0:T(1,128)}) custom-call(bf16[4,4,8,32]{3,2,1,0:T(8,128)(2,1)} %get-tuple-element.11.act_in, bf16[4,4,8,32]{3,2,1,0:T(8,128)(2,1)} %get-tuple-element.12.ig_in, bf16[32,16,128]{2,1,0:T(8,128)(2,1)} %get-tuple-element.13.total), custom_call_target="tpu_custom_call" | custom-call | tf_op jit(solution)/shard_map/pallas_call | solution.py:416

commit v5 on v4

--- a/solution.py
+++ b/solution.py
@@ -64,7 +64,7 @@
 
     loads[0].wait()
     for x in range(4):
-        planes[x] = joined(x_ref, x)
+        planes[x] = joined(x_ref, x).astype(BF16)
 
     pl.semaphore_wait(barrier, 4 + len(HALO))
 
@@ -122,10 +122,10 @@
     def beside(plane, dy):
         if plane == 0 or plane == 5:
             dx = -1 if plane == 0 else 1
-            return guarded(rim[HALO.index((-dx, -dy)), 0], -dx, -dy)
+            return guarded(rim[HALO.index((-dx, -dy)), 0].astype(F32), -dx, -dy)
         if dy == 0:
-            return planes[plane - 1]
-        return guarded(rim[HALO.index((0, -dy)), plane - 1], 0, -dy)
+            return planes[plane - 1].astype(F32)
+        return guarded(rim[HALO.index((0, -dy)), plane - 1].astype(F32), 0, -dy)
 
     shifted = {}
     for plane in range(6):
@@ -373,15 +373,15 @@
     size = 256 // peers
     factor = 1.0 / math.sqrt(512 * peers)
     vmem = pl.BlockSpec(memory_space=pltpu.VMEM)
-    hbm = pl.BlockSpec(memory_space=pl.ANY)
+    anywhere = pl.BlockSpec(memory_space=pl.ANY)
     sems = [(8,)] * 2 + [(4, 2)] * 2 + [(groups,)] * 4 + [(4,)] * 2 + [()] * 4 + [(8,)] * 2
     cells = jax.ShapeDtypeStruct((4, 4, 8, 32), BF16)
     gathered = jax.ShapeDtypeStruct((peers, 2 * size, chans // 2), BF16)
     results = pl.pallas_call(
         functools.partial(kernel, nx, ny, nz, factor),
         out_shape=(cells, cells, gathered),
-        in_specs=[hbm] * 4,
-        out_specs=(hbm,) * 3,
+        in_specs=[pl.BlockSpec(memory_space=pltpu.HBM)] * 4,
+        out_specs=(anywhere,) * 3,
         scratch_shapes=[
             pltpu.VMEM((4, 4, 8, 32), BF16),
             pltpu.VMEM((216, chans), BF16),
@@ -389,8 +389,8 @@
             pltpu.VMEM((4, 4, 8, 32), BF16),
             pltpu.VMEM((4, 4, 8, 32), BF16),
             pltpu.VMEM((4, 4, 8, 32), BF16),
-            pltpu.VMEM((4, 8, 128), F32),
-            pltpu.VMEM((8, 4, 8, 128), F32),
+            pltpu.VMEM((4, 8, 128), BF16),
+            pltpu.VMEM((8, 4, 8, 128), BF16),
             pltpu.VMEM((CLASSES, groups, 16, 256), BF16),
             pltpu.VMEM((4, groups, 16, 256), BF16),
             pltpu.VMEM((groups, 16, 256), BF16),
@@ -406,17 +406,23 @@
             pltpu.SemaphoreType.REGULAR((8,)),
         ]
         + [pltpu.SemaphoreType.DMA(n) for n in sems],
-        compiler_params=pltpu.CompilerParams(collective_id=0, has_side_effects=True),
+        compiler_params=pltpu.CompilerParams(collective_id=0, has_side_effects=True, vmem_limit_bytes=16 << 20),
     )(
-        jnp.transpose(inputs, (0, 1, 3, 2)),
-        weight.reshape(216, chans),
-        bias.reshape(1, 8),
-        jnp.transpose(cotangent, (0, 1, 3, 2)),
+        *(
+            pltpu.with_memory_space_constraint(array, pltpu.HBM)
+            for array in (
+                jnp.transpose(inputs, (0, 1, 3, 2)),
+                weight.reshape(216, chans),
+                bias.reshape(1, 8),
+                jnp.transpose(cotangent, (0, 1, 3, 2)),
+            )
+        )
     )
     act, grad_in, grad_w, grad_b = pl.pallas_call(
         functools.partial(hand_on, size),
         out_shape=(cells, cells, jax.ShapeDtypeStruct((216, chans), F32), jax.ShapeDtypeStruct((1, 8), F32)),
         in_specs=[vmem] * 3,
+        compiler_params=pltpu.CompilerParams(vmem_limit_bytes=8 << 20),
         out_specs=(vmem,) * 4,
     )(*results)
     return (

time: 72.4 us -> 71.3 us (0.985)
  Pallas kernels: 71.6 us -> 70.5 us
    pallas_call x1, Pallas kernels: 1.66 us -> 0.72 us  [body(): pl.pallas_call(functools.partial(hand_on, size), out_shape=(cells, cells,...]
where the time goes in v5:
time: 71.3 us; the launch traced here: 71.2 us
  Pallas kernels  70.5 us (99%)
    pallas_call x1, Pallas kernels, body(): pl.pallas_call(functools.partial(kernel, nx, ny, nz, factor), out_shape=(...  69.8 us

profile of v5, /device:TPU:1, one launch (start us, length us, event | category | flops | bytes accessed | tf_op | source)
XLA Modules:
  0.0 71.2 jit_solution(13905572508345556641)
XLA Ops:
  0.6 69.8 %shard_map.75 = (bf16[4,4,8,32]{3,2,1,0:T(8,128)(2,1)S(1)}, bf16[4,4,8,32]{3,2,1,0:T(8,128)(2,1)S(1)}, bf16[32,16,128]{2,1,0:T(8,128)(2,1)S(1)}) custom-call(bf16[4,4,8,32]{3,2,1,0:T(8,128)(2,1)} %bitcast.9, bf16[216,256]{1,0:T(8,128)(2,1)} %bitcast.8, bf16[1,8]{1,0:T(2,128)(2,1)} %bitcast.11, bf16[4,4,8,32]{3,2,1,0:T(8,128)(2,1)} %bitcast.10), custom_call_target="tpu_custom_call" | custom-call | tf_op jit(solution)/shard_map/pallas_call | solution.py:380
  70.4 0.7 %shard_map.76 = (bf16[4,4,8,32]{3,2,1,0:T(8,128)(2,1)}, bf16[4,4,8,32]{3,2,1,0:T(8,128)(2,1)}, f32[216,256]{1,0:T(8,128)}, f32[1,8]{1,0:T(1,128)}) custom-call(bf16[4,4,8,32]{3,2,1,0:T(8,128)(2,1)S(1)} %get-tuple-element.11.act_in, bf16[4,4,8,32]{3,2,1,0:T(8,128)(2,1)S(1)} %get-tuple-element.12.ig_in, bf16[32,16,128]{2,1,0:T(8,128)(2,1)S(1)} %get-tuple-element.13.total), custom_call_target="tpu_custom_call" | custom-call | tf_op jit(solution)/shard_map/pallas_call | solution.py:421
